TPU v7x, 32 devices: a whole 2x2x4 slice. The times are simulated.
32 devices in a mesh: pts: 8 (over z, y), feat: 4 (over x, core).
Axes of the slice: x: 2, y: 2, z: 4, core: 2. Of those that a mesh axis runs over, the one named last changes fastest.
Arguments:
- slab: bfloat16 [16384, 768], P('pts', 'feat'), may hold values from -40 to 40
- centres: bfloat16 [4096, 768], replicated, may hold values from -3 to 3
- labels: int32 [16384, 1], P(('pts', 'feat')), may hold values from 0 to 4095
- sample_rows: int32 [8, 8, 4], P('pts'), may hold values from 0 to 2047, as said below
- sample_count: int32 [8, 8], P('pts'), may hold values from 0 to 4, as said below
- slot_offset: int32 [8, 8], P('pts'), may hold values from 0 to 28, as said below
Outputs:
- coreset: bfloat16 [256, 768], P('pts', 'feat')
Inputs may be any that keep to these rules, and one draw needn't show every extreme that they name: `sample_rows`: row indices within a source shard; sampled independently with replacement. `sample_count`: in every draw some owner receives 4 rows from every source. slot_offset[o,p] is the sum of sample_count[q,o] over sources q < p.
All inputs are finite; a program needn't handle non-finite values.
Results may differ from a plain program's by a relative error of at most 0.0006.
Values may be sent and summed in bfloat16 or wider, within the bound.
A program may use at most 64 MiB of HBM per device.

v0:
```python
import jax
import jax.numpy as jnp
from jax import lax
from jax.sharding import PartitionSpec as P


def local(slab, centres, labels, sample_rows, sample_count, slot_offset):
    rows_pts, feat_width = slab.shape
    feat_count = lax.axis_size("feat")
    rows_dev = rows_pts // feat_count
    centre_count = centres.shape[0]
    contract = (((1,), (1,)), ((), ()))
    centre_sq = jnp.sum(jnp.square(centres.astype(jnp.float32)), axis=1)
    stacked = slab.reshape(feat_count, rows_dev, feat_width)
    points = lax.all_to_all(stacked, "feat", split_axis=0, concat_axis=2, tiled=True)[0]
    cross_term = lax.dot_general(points, centres, contract, preferred_element_type=jnp.float32)
    point_sq = jnp.sum(jnp.square(points.astype(jnp.float32)), axis=1)
    nearest = jnp.min(point_sq[:, None] + centre_sq[None, :] - 2.0 * cross_term, axis=1)[None, :][0]
    member = labels[:, 0]
    cost_part = jax.ops.segment_sum(nearest, member, num_segments=centre_count)
    size_part = jax.ops.segment_sum(jnp.ones_like(nearest), member, num_segments=centre_count)
    cluster_cost, cluster_size = lax.psum((cost_part, size_part), ("pts", "feat"))
    own_sens = nearest / jnp.take(cluster_cost, member) + 1.0 / jnp.take(cluster_size, member)
    shard_sens = lax.all_gather(own_sens, "feat", axis=0, tiled=True)
    total_points = rows_pts * lax.axis_size("pts")
    weight = 2.0 * centre_count / total_points / shard_sens
    picked_rows = sample_rows[0]
    owner_count, slot_count = picked_rows.shape
    chosen = jnp.take(slab, picked_rows.reshape(-1), axis=0).reshape(
        owner_count, slot_count, feat_width
    )
    chosen_weight = jnp.take(weight, picked_rows)
    live_slot = jnp.arange(slot_count, dtype=jnp.int32)[None, :] < sample_count[0][:, None]
    scaled = jnp.where(
        live_slot[:, :, None], chosen.astype(jnp.float32) * chosen_weight[:, :, None], 0.0
    ).astype(jnp.bfloat16)
    arrived = lax.all_to_all(scaled, "pts", split_axis=0, concat_axis=0, tiled=True)
    target = slot_offset[0][:, None] + jnp.arange(slot_count, dtype=jnp.int32)[None, :]
    own_rows = arrived.shape[0] * slot_count
    placed = jnp.zeros((own_rows, feat_width), jnp.float32)
    placed = placed.at[target.reshape(-1)].add(
        arrived.reshape(-1, feat_width).astype(jnp.float32), mode="drop"
    )
    return placed.astype(jnp.bfloat16)


def solution(mesh):
    placed = (
        P("pts", "feat"),
        P(),
        P(("pts", "feat"), None),
        P("pts", None, None),
        P("pts", None),
        P("pts", None),
    )
    return jax.shard_map(
        local, mesh=mesh, in_specs=placed, out_specs=P("pts", "feat"), check_vma=False
    )
```

profile of v0, /device:TPU:0, one launch (start us, length us, event | category | flops | bytes accessed | tf_op | source)
XLA Modules:
  0.0 99.5 jit_solution(1397401444950790253)
XLA Ops:
  0.0 2.1 %copy.35 = bf16[24,4,8,512]{3,2,0,1:T(8,128)(2,1)} copy(bf16[24,4,8,512]{3,2,1,0:T(8,128)(2,1)} %bitcast.31) | data formatting | bytes 1572864 | tf_op jit(solution)/shard_map/reshape | solution.py:14
  2.1 4.2 %all-to-all-start = ((bf16[4,512,192]{1,2,0:T(8,128)(2,1)}), bf16[4,512,192]{1,2,0:T(8,128)(2,1)S(1)}, u32[]{:S(2)}, u32[]{:S(2)}) async-start(bf16[4,512,192]{1,2,0:T(8,128)(2,1)} %bitcast.29), calls=%async_computation | async-start | bytes 1572864 | tf_op jit(solution)/shard_map/all_to_all | solution.py:15
  6.3 1.4 %copy.28 = bf16[2048,192]{1,0:T(8,128)(2,1)S(1)} copy(bf16[2048,192]{0,1:T(8,128)(2,1)} %param.8) | data formatting | bytes 1572864 | tf_op args[0]
  7.8 0.7 compare_select_fusion.1
  8.4 0.8 copy.27
  9.2 0.7 compare_select_fusion
  9.9 0.1 copy.30
  10.0 0.1 reshape.185
  10.1 0.1 reshape_squeeze.6
  10.2 0.6 gather_fusion
  10.8 0.7 iota_compare_fusion
  11.5 0.7 iota_add_fusion
  12.3 0.1 add.119
  12.3 3.4 %scatter_custom_fusion.1 = f32[4096]{0:T(1024)S(1)} fusion(s32[512]{0:T(512)} %bitcast.35, f32[512]{0:T(512)S(1)} %broadcast.113, f32[]{:T(128)} %constant.22.clone.1), kind=kCustom, calls=%fused_computation.14 | custom fusion | flops 512 | bytes 16896 | tf_op jit(solution)/shard_map/scatter-add | solution.py:21
  15.8 4.1 %multiply_reduce_fusion = f32[4096]{0:T(1024)S(1)} fusion(bf16[4096,768]{1,0:T(8,128)(2,1)} %param.9), kind=kLoop, calls=%fused_computation.7 | loop fusion | flops 9433088 | bytes 6307840 | tf_op jit(solution)/shard_map/reduce_sum | solution.py:13
  19.9 0.2 multiply_reduce_fusion.1
  20.1 7.5 %subtract_reduce_fusion = f32[512]{0:T(512)S(1)} fusion(bf16[512,768]{0,1:T(8,128)(2,1)S(1)} %bitcast.32, bf16[4096,768]{1,0:T(8,128)(2,1)} %param.9, f32[4096]{0:T(1024)S(1)} %multiply_reduce_fusion, f32[512]{0:T(512)S(1)} %multiply_reduce_fusion.1), kind=kOutput, calls=%fused_computation.8 | convolution fusion | flops 3229613568 | bytes 7098368 | tf_op jit(solution)/shard_map/dot_general | solution.py:16
  27.6 3.3 %scatter_custom_fusion = f32[4096]{0:T(1024)S(1)} fusion(s32[512]{0:T(512)S(1)} %bitcast.36, f32[512]{0:T(512)S(1)} %subtract_reduce_fusion, f32[]{:T(128)} %constant.22.clone.1), kind=kCustom, calls=%fused_computation.16 | custom fusion | flops 512 | bytes 16388 | tf_op jit(solution)/shard_map/scatter-add | solution.py:20
  30.9 42.0 %all-reduce = (f32[4096]{0:T(1024)S(1)}, f32[4096]{0:T(1024)S(1)}) all-reduce(f32[4096]{0:T(1024)S(1)} %scatter_custom_fusion.1, f32[4096]{0:T(1024)S(1)} %scatter_custom_fusion), channel_id=1, replica_groups=mesh['pts'=8,'feat'=4] {'pts','feat'}, use_global_device_ids=true, to_apply=%region_6.8 | all-reduce | flops 8192 | bytes 65536 | tf_op jit(solution)/shard_map/psum | solution.py:22
  72.9 3.1 %gather_fusion.2 = f32[512]{0:T(512)S(1)} fusion(f32[4096]{0:T(1024)S(1)} %get-tuple-element.7, s32[1024]{0:T(1024)S(1)} %pad_clamp_fusion.1), kind=kCustom, calls=%fused_computation.clone | custom fusion | bytes 6144 | tf_op jit(solution)/shard_map/jit(_take)/gather | solution.py:23
  76.0 3.1 %gather_fusion.3 = f32[512]{0:T(512)S(1)} fusion(f32[4096]{0:T(1024)S(1)} %get-tuple-element.6, s32[1024]{0:T(1024)S(1)} %pad_clamp_fusion.1), kind=kCustom, calls=%fused_computation.1.clone | custom fusion | bytes 6144 | tf_op jit(solution)/shard_map/jit(_take)/gather | solution.py:23
  79.2 5.5 %all-gather = f32[4,1,512]{2,1,0:T(1,128)S(1)} all-gather(f32[1,1,512]{2,1,0:T(1,128)S(1)} %bitcast.33), channel_id=1, replica_groups=mesh['pts'=8,'feat'=4] {'feat'}, dimensions={0}, use_global_device_ids=true | all-gather | bytes 10240 | tf_op jit(solution)/shard_map/all_gather | solution.py:24
  84.7 0.7 gather_fusion.1
  85.4 0.1 reshape.184
  85.4 0.1 copy.31
  85.5 0.1 copy.32
  85.6 0.1 copy.26
  85.7 0.7 select_convert_fusion
  86.4 5.1 %all-to-all-start.1 = ((bf16[8,4,192]{2,1,0:T(4,128)(2,1)}), bf16[8,4,192]{2,1,0:T(4,128)(2,1)S(1)}, u32[]{:S(2)}, u32[]{:S(2)}) async-start(bf16[8,4,192]{2,1,0:T(4,128)(2,1)} %select_convert_fusion), calls=%async_computation.1 | async-start | bytes 32768 | tf_op jit(solution)/shard_map/all_to_all | solution.py:37
  91.5 6.6 %all-to-all-done.1 = bf16[8,4,192]{2,1,0:T(4,128)(2,1)S(1)} async-done(((bf16[8,4,192]{2,1,0:T(4,128)(2,1)}), bf16[8,4,192]{2,1,0:T(4,128)(2,1)S(1)}, u32[]{:S(2)}, u32[]{:S(2)}) %all-to-all-start.1) | async-done | bytes 12320 | tf_op jit(solution)/shard_map/all_to_all | solution.py:37
  98.1 0.8 scatter_custom_fusion.2
  98.9 0.6 convert_element_type.28
  (16 shorter events, 0.1 us)
Async XLA Ops:
  2.1 17.8 %all-to-all-start = ((bf16[4,512,192]{1,2,0:T(8,128)(2,1)}), bf16[4,512,192]{1,2,0:T(8,128)(2,1)S(1)}, u32[]{:S(2)}, u32[]{:S(2)}) async-start(bf16[4,512,192]{1,2,0:T(8,128)(2,1)} %bitcast.29), calls=%async_computation | async-start | bytes 1572864 | tf_op jit(solution)/shard_map/all_to_all | solution.py:15
  20.1 7.5 %copy-start.1 = (s32[512,1]{0,1:T(1,128)S(1)}, s32[512,1]{0,1:T(1,128)}, u32[]{:S(2)}) copy-start(s32[512,1]{0,1:T(1,128)} %param.10) | copy-start | bytes 6148
  27.6 57.9 %copy-start = (s32[1,8,4]{1,2,0:T(4,128)S(1)}, s32[1,8,4]{1,2,0:T(4,128)}, u32[]{:S(2)}) copy-start(s32[1,8,4]{1,2,0:T(4,128)} %param.11) | copy-start | bytes 388
  86.4 11.6 %all-to-all-start.1 = ((bf16[8,4,192]{2,1,0:T(4,128)(2,1)}), bf16[8,4,192]{2,1,0:T(4,128)(2,1)S(1)}, u32[]{:S(2)}, u32[]{:S(2)}) async-start(bf16[8,4,192]{2,1,0:T(4,128)(2,1)} %select_convert_fusion), calls=%async_computation.1 | async-start | bytes 32768 | tf_op jit(solution)/shard_map/all_to_all | solution.py:37
where the time goes:
time: 100 us; the launch traced here: 99.5 us
  blocking collectives  47.4 us (47%)
  other arithmetic  15.9 us (16%)
  local copies, waits for them, and re-layouts  12.6 us (13%)
  starting transfers between devices  9.3 us (9%)
  matrix products  7.52 us (8%)
  waiting for transfers between devices  6.57 us (7%)
    psum x1, blocking collectives, local(): lax.psum((cost_part, size_part), ('pts', 'feat'))  42 us
    dot_general x1, matrix products, local(): lax.dot_general(points, centres, contract, preferred_element_type=jnp.flo...  7.52 us
    all_to_all x1, waiting for transfers between devices, local(): lax.all_to_all(scaled, 'pts', split_axis=0, concat_axis=0, tiled=True)  6.57 us
    all_gather x1, blocking collectives, local(): shard_sens = lax.all_gather(own_sens, 'feat', axis=0, tiled=True)  5.45 us
    all_to_all x1, starting transfers between devices, local(): lax.all_to_all(scaled, 'pts', split_axis=0, concat_axis=0, tiled=True)  5.07 us
    all_to_all x1, starting transfers between devices, local(): lax.all_to_all(stacked, 'feat', split_axis=0, concat_axis=2, tiled=True)[0]  4.24 us
    reduce_sum x1, other arithmetic, local(): centre_sq = jnp.sum(jnp.square(centres.astype(jnp.float32)), axis=1)  4.09 us
    scatter-add x1, other arithmetic, local(): jax.ops.segment_sum(jnp.ones_like(nearest), member, num_segments=centre_c...  3.39 us
  transfers between devices with their start and end apart: 2, of which 1 were waited for; matrix products, arithmetic and copies ran while one was open for 14% of the time, Pallas kernels for 0%

commit v1 on v0

--- a/solution.py
+++ b/solution.py
@@ -21,7 +21,23 @@
     size_part = jax.ops.segment_sum(jnp.ones_like(nearest), member, num_segments=centre_count)
     cluster_cost, cluster_size = lax.psum((cost_part, size_part), ("pts", "feat"))
     own_sens = nearest / jnp.take(cluster_cost, member) + 1.0 / jnp.take(cluster_size, member)
-    shard_sens = lax.all_gather(own_sens, "feat", axis=0, tiled=True)
+    ways, here, step = (lax.axis_size("feat"), lax.axis_index("feat"), own_sens.shape[0])
+    shape = [n * ways if d == 0 else n for d, n in enumerate(own_sens.shape)]
+    full = lax.dynamic_update_slice_in_dim(
+        jnp.zeros(shape, own_sens.dtype), own_sens, here * step, axis=0
+    )
+    going_up = going_down = own_sens
+    for far in range(1, ways // 2 + 1):
+        going_up = lax.ppermute(going_up, "feat", [(d, (d + 1) % ways) for d in range(ways)])
+        full = lax.dynamic_update_slice_in_dim(full, going_up, (here - far) % ways * step, axis=0)
+        if 2 * far < ways:
+            going_down = lax.ppermute(
+                going_down, "feat", [(d, (d - 1) % ways) for d in range(ways)]
+            )
+            full = lax.dynamic_update_slice_in_dim(
+                full, going_down, (here + far) % ways * step, axis=0
+            )
+    shard_sens = full
     total_points = rows_pts * lax.axis_size("pts")
     weight = 2.0 * centre_count / total_points / shard_sens
     picked_rows = sample_rows[0]

time: 100 us -> 99 us (0.990)
  blocking collectives: 47.4 us -> 41.7 us
  waiting for transfers between devices: 6.57 us -> 9.35 us
  starting transfers between devices: 9.3 us -> 11.4 us
    all_gather x1 -> x0, blocking collectives: 5.45 us -> none  [local(): shard_sens = lax.all_gather(own_sens, 'feat', axis=0, tiled=True)]
    ppermute x0 -> x3, waiting for transfers between devices: none -> 2.49 us  [the longest x2 2.49 us: local(): lax.ppermute(going_up, 'feat', [(d, (d + 1) % ways) for d in range(ways)])]
    ppermute x0 -> x3, starting transfers between devices: none -> 1.8 us  [the longest x1 1.7 us: local(): lax.ppermute(going_down, 'feat', [(d, (d - 1) % ways) for d in range(ways)])]
    unnamed x6 -> x8, local copies, waits for them, and re-layouts: 2.19 us -> 1.27 us
  transfers between devices with their start and end apart: 2 -> 5, of which waited for: 1 -> 4; matrix products, arithmetic and copies ran while one was open for 14% -> 13% of each run, Pallas kernels for 0% -> 0%
where the time goes in v1:
time: 99 us; the launch traced here: 98.5 us
  blocking collectives  41.7 us (42%)
  other arithmetic  16 us (16%)
  local copies, waits for them, and re-layouts  12.3 us (12%)
  starting transfers between devices  11.4 us (12%)
  waiting for transfers between devices  9.35 us (9%)
  matrix products  7.58 us (8%)
    psum x1, blocking collectives, local(): lax.psum((cost_part, size_part), ('pts', 'feat'))  41.7 us
    dot_general x1, matrix products, local(): lax.dot_general(points, centres, contract, preferred_element_type=jnp.flo...  7.58 us
    all_to_all x1, waiting for transfers between devices, local(): lax.all_to_all(scaled, 'pts', split_axis=0, concat_axis=0, tiled=True)  6.57 us
    all_to_all x1, starting transfers between devices, local(): lax.all_to_all(scaled, 'pts', split_axis=0, concat_axis=0, tiled=True)  5.33 us
    all_to_all x1, starting transfers between devices, local(): lax.all_to_all(stacked, 'feat', split_axis=0, concat_axis=2, tiled=True)[0]  4.24 us
    reduce_sum x1, other arithmetic, local(): centre_sq = jnp.sum(jnp.square(centres.astype(jnp.float32)), axis=1)  4.09 us
    scatter-add x1, other arithmetic, local(): jax.ops.segment_sum(jnp.ones_like(nearest), member, num_segments=centre_c...  3.39 us
    scatter-add x1, other arithmetic, local(): cost_part = jax.ops.segment_sum(nearest, member, num_segments=centre_count)  3.26 us
  transfers between devices with their start and end apart: 5, of which 4 were waited for; matrix products, arithmetic and copies ran while one was open for 13% of the time, Pallas kernels for 0%

profile of v1, /device:TPU:0, one launch (start us, length us, event | category | flops | bytes accessed | tf_op | source)
XLA Modules:
  0.0 98.5 jit_solution(893397196803037768)
XLA Ops:
  0.0 2.1 %copy.35 = bf16[24,4,8,512]{3,2,0,1:T(8,128)(2,1)} copy(bf16[24,4,8,512]{3,2,1,0:T(8,128)(2,1)} %bitcast.28) | data formatting | bytes 1572864 | tf_op jit(solution)/shard_map/reshape | solution.py:14
  2.1 4.2 %all-to-all-start = ((bf16[4,512,192]{1,2,0:T(8,128)(2,1)}), bf16[4,512,192]{1,2,0:T(8,128)(2,1)S(1)}, u32[]{:S(2)}, u32[]{:S(2)}) async-start(bf16[4,512,192]{1,2,0:T(8,128)(2,1)} %bitcast.27), calls=%async_computation | async-start | bytes 1572864 | tf_op jit(solution)/shard_map/all_to_all | solution.py:15
  6.3 0.7 compare_select_fusion.1
  7.0 0.8 copy.27
  7.8 0.7 compare_select_fusion
  8.7 0.7 iota_compare_fusion
  9.4 0.7 iota_add_fusion
  10.2 3.4 %scatter_custom_fusion.1 = f32[4096]{0:T(1024)S(1)} fusion(s32[512]{0:T(512)} %bitcast.31, f32[512]{0:T(512)S(1)} %broadcast.116, f32[]{:T(128)} %constant.48.clone.1), kind=kCustom, calls=%fused_computation.14 | custom fusion | flops 512 | bytes 16896 | tf_op jit(solution)/shard_map/scatter-add | solution.py:21
  13.6 4.1 %multiply_reduce_fusion = f32[4096]{0:T(1024)S(1)} fusion(bf16[4096,768]{1,0:T(8,128)(2,1)} %param.9), kind=kLoop, calls=%fused_computation.7 | loop fusion | flops 9433088 | bytes 6307840 | tf_op jit(solution)/shard_map/reduce_sum | solution.py:13
  17.7 0.3 all-to-all-done
  17.9 0.2 multiply_reduce_fusion.1
  18.2 7.6 %subtract_reduce_fusion = f32[512]{0:T(512)S(1)} fusion(bf16[512,768]{0,1:T(8,128)(2,1)S(1)} %bitcast.29, bf16[4096,768]{1,0:T(8,128)(2,1)} %param.9, f32[4096]{0:T(1024)S(1)} %multiply_reduce_fusion, f32[512]{0:T(512)S(1)} %multiply_reduce_fusion.1), kind=kOutput, calls=%fused_computation.8 | convolution fusion | flops 3229613568 | bytes 7098368 | tf_op jit(solution)/shard_map/dot_general | solution.py:16
  25.8 3.3 %scatter_custom_fusion = f32[4096]{0:T(1024)S(1)} fusion(s32[512]{0:T(512)S(1)} %bitcast.32, f32[512]{0:T(512)S(1)} %subtract_reduce_fusion, f32[]{:T(128)} %constant.48.clone.1), kind=kCustom, calls=%fused_computation.16 | custom fusion | flops 512 | bytes 16388 | tf_op jit(solution)/shard_map/scatter-add | solution.py:20
  29.0 41.7 %all-reduce = (f32[4096]{0:T(1024)S(1)}, f32[4096]{0:T(1024)S(1)}) all-reduce(f32[4096]{0:T(1024)S(1)} %scatter_custom_fusion.1, f32[4096]{0:T(1024)S(1)} %scatter_custom_fusion), channel_id=1, replica_groups=mesh['pts'=8,'feat'=4] {'pts','feat'}, use_global_device_ids=true, to_apply=%region_6.8 | all-reduce | flops 8192 | bytes 65536 | tf_op jit(solution)/shard_map/psum | solution.py:22
  70.8 3.1 %gather_fusion.2 = f32[512]{0:T(512)S(1)} fusion(f32[4096]{0:T(1024)S(1)} %get-tuple-element.7, s32[1024]{0:T(1024)S(1)} %pad_clamp_fusion.1), kind=kCustom, calls=%fused_computation.clone | custom fusion | bytes 6144 | tf_op jit(solution)/shard_map/jit(_take)/gather | solution.py:23
  73.9 3.1 %gather_fusion.3 = f32[512]{0:T(512)S(1)} fusion(f32[4096]{0:T(1024)S(1)} %get-tuple-element.6, s32[1024]{0:T(1024)S(1)} %pad_clamp_fusion.1), kind=kCustom, calls=%fused_computation.1.clone | custom fusion | bytes 6144 | tf_op jit(solution)/shard_map/jit(_take)/gather | solution.py:23
  77.1 0.1 fusion.8
  77.3 1.7 %collective-permute-start.1 = (f32[512]{0:T(512)S(1)}, f32[512]{0:T(512)S(1)}, u32[]{:S(2)}, u32[]{:S(2)}) collective-permute-start(f32[512]{0:T(512)S(1)} %get-tuple-element.11), channel_id=1, source_target_pairs={{0,3},{1,0},{2,1},{3,2},{4,7},{5,4},{6,5},{7,6},{8,11},{9,8},{10,9... | collective-permute-start | bytes 6152 | tf_op jit(solution)/shard_map/ppermute | solution.py:34
  79.0 1.3 %collective-permute-done = f32[512]{0:T(512)S(1)} collective-permute-done((f32[512]{0:T(512)S(1)}, f32[512]{0:T(512)S(1)}, u32[]{:S(2)}, u32[]{:S(2)}) %collective-permute-start) | collective-permute-done | bytes 2080 | tf_op jit(solution)/shard_map/ppermute | solution.py:31
  80.3 0.5 copy.28
  80.8 0.6 gather_fusion
  81.6 0.2 dynamic_update_slice.13
  81.8 0.2 dynamic_update_slice.14
  82.0 1.2 %collective-permute-done.2 = f32[512]{0:T(512)S(1)} collective-permute-done((f32[512]{0:T(512)S(1)}, f32[512]{0:T(512)S(1)}, u32[]{:S(2)}, u32[]{:S(2)}) %collective-permute-start.2) | collective-permute-done | bytes 2080 | tf_op jit(solution)/shard_map/ppermute | solution.py:31
  83.2 0.2 dynamic_update_slice.15
  83.4 0.7 gather_fusion.1
  84.4 0.1 copy.26
  84.5 0.7 select_convert_fusion
  85.2 5.3 %all-to-all-start.1 = ((bf16[8,4,192]{2,1,0:T(4,128)(2,1)}), bf16[8,4,192]{2,1,0:T(4,128)(2,1)S(1)}, u32[]{:S(2)}, u32[]{:S(2)}) async-start(bf16[8,4,192]{2,1,0:T(4,128)(2,1)} %select_convert_fusion), calls=%async_computation.1 | async-start | bytes 32768 | tf_op jit(solution)/shard_map/all_to_all | solution.py:53
  90.5 6.6 %all-to-all-done.1 = bf16[8,4,192]{2,1,0:T(4,128)(2,1)S(1)} async-done(((bf16[8,4,192]{2,1,0:T(4,128)(2,1)}), bf16[8,4,192]{2,1,0:T(4,128)(2,1)S(1)}, u32[]{:S(2)}, u32[]{:S(2)}) %all-to-all-start.1) | async-done | bytes 12320 | tf_op jit(solution)/shard_map/all_to_all | solution.py:53
  97.1 0.8 scatter_custom_fusion.2
  97.9 0.6 convert_element_type.28
  (27 shorter events, 0.8 us)
Async XLA Ops:
  2.1 15.9 %all-to-all-start = ((bf16[4,512,192]{1,2,0:T(8,128)(2,1)}), bf16[4,512,192]{1,2,0:T(8,128)(2,1)S(1)}, u32[]{:S(2)}, u32[]{:S(2)}) async-start(bf16[4,512,192]{1,2,0:T(8,128)(2,1)} %bitcast.27), calls=%async_computation | async-start | bytes 1572864 | tf_op jit(solution)/shard_map/all_to_all | solution.py:15
  18.2 7.6 %copy-start.2 = (s32[512,1]{0,1:T(1,128)S(1)}, s32[512,1]{0,1:T(1,128)}, u32[]{:S(2)}) copy-start(s32[512,1]{0,1:T(1,128)} %param.10) | copy-start | bytes 6148
  18.2 62.2 %copy-start = (bf16[2048,192]{0,1:T(8,128)(2,1)S(1)}, bf16[2048,192]{0,1:T(8,128)(2,1)}, u32[]{:S(2)}) copy-start(bf16[2048,192]{0,1:T(8,128)(2,1)} %param.8) | copy-start | bytes 2359300
  25.8 58.5 %copy-start.1 = (s32[1,8,4]{1,2,0:T(4,128)S(1)}, s32[1,8,4]{1,2,0:T(4,128)}, u32[]{:S(2)}) copy-start(s32[1,8,4]{1,2,0:T(4,128)} %param.11) | copy-start | bytes 388
  77.2 3.0 %collective-permute-start = (f32[512]{0:T(512)S(1)}, f32[512]{0:T(512)S(1)}, u32[]{:S(2)}, u32[]{:S(2)}) collective-permute-start(f32[512]{0:T(512)S(1)} %get-tuple-element.11), channel_id=1, source_target_pairs={{0,1},{1,2},{2,3},{3,0},{4,5},{5,6},{6,7},{7,4},{8,9},{9,10},{10,1... | collective-permute-start | bytes 6152 | tf_op jit(solution)/shard_map/ppermute | solution.py:31
  77.3 4.5 %collective-permute-start.1 = (f32[512]{0:T(512)S(1)}, f32[512]{0:T(512)S(1)}, u32[]{:S(2)}, u32[]{:S(2)}) collective-permute-start(f32[512]{0:T(512)S(1)} %get-tuple-element.11), channel_id=1, source_target_pairs={{0,3},{1,0},{2,1},{3,2},{4,7},{5,4},{6,5},{7,6},{8,11},{9,8},{10,9... | collective-permute-start | bytes 6152 | tf_op jit(solution)/shard_map/ppermute | solution.py:34
  80.2 3.0 %collective-permute-start.2 = (f32[512]{0:T(512)S(1)}, f32[512]{0:T(512)S(1)}, u32[]{:S(2)}, u32[]{:S(2)}) collective-permute-start(f32[512]{0:T(512)S(1)} %collective-permute-done), channel_id=1, source_target_pairs={{0,1},{1,2},{2,3},{3,0},{4,5},{5,6},{6,7},{7,4},{8,9},{9,10},{10,1... | collective-permute-start | bytes 6152 | tf_op jit(solution)/shard_map/ppermute | solution.py:31
  85.2 11.9 %all-to-all-start.1 = ((bf16[8,4,192]{2,1,0:T(4,128)(2,1)}), bf16[8,4,192]{2,1,0:T(4,128)(2,1)S(1)}, u32[]{:S(2)}, u32[]{:S(2)}) async-start(bf16[8,4,192]{2,1,0:T(4,128)(2,1)} %select_convert_fusion), calls=%async_computation.1 | async-start | bytes 32768 | tf_op jit(solution)/shard_map/all_to_all | solution.py:53
